TPU v7x, 256 devices: a whole 4x4x8 slice. The times are simulated.
256 devices in a mesh: tile: 4 (over y), proj: 16 (over x, z_hi, core), cuts: 4 (over z_lo).
Axes of the slice: x: 4, y: 4, z: 8 (z_hi: 2, z_lo: 4; z = z_hi * 4 + z_lo), core: 2. Of those that a mesh axis runs over, the one named last changes fastest.
Arguments:
- object_field: float32 [64, 2, 384, 2048], P(('proj', 'cuts'), None, None, 'tile'), may hold values from -5 to 5
- probe_field: float32 [2, 256, 256], replicated, may hold values from -6 to 6
- amplitudes: bfloat16 [64, 4, 6, 256, 256], P(('proj', 'cuts'), 'tile'), may hold values from 0 to 16
- pos_rows: int32 [64, 4, 6], P(('proj', 'cuts'), 'tile'), may hold values from 0 to 128
- pos_cols: int32 [64, 4, 6], P(('proj', 'cuts'), 'tile'), may hold values from 0 to 512
- counts: int32 [64, 4], P(('proj', 'cuts'), 'tile'), may hold values from 1 to 6, as said below
- admm_dual: float32 [64, 32, 2048], P(('proj', 'cuts'), None, 'tile'), may hold values from -4 to 4
- volume: float32 [32, 2048, 2048], P('cuts', ('tile', 'proj')), may hold values from -6 to 6
- proj_weights: bfloat16 [16, 2048, 2048], P(None, ('tile', 'proj')), may hold values from -0.125 to 0.125
- ray_weights: float32 [16, 2048], replicated, may hold values from -0.125 to 0.125
- angle_ids: int32 [64], replicated, may hold values from 0 to 15
Outputs:
- new_object: float32 [64, 2, 384, 2048], P(('proj', 'cuts'), None, None, 'tile')
- new_probe: float32 [2, 256, 256], replicated
- new_volume: float32 [32, 2048, 2048], P('cuts', ('tile', 'proj'))
Inputs may be any that keep to these rules, and one draw needn't show every extreme that they name: `counts`: every tile holds at least one live position and at most 6; exactly one tile of one projection holds 6, every other holds at most 3.
All inputs are finite; a program needn't handle non-finite values.
Results may differ from a plain program's by a relative error of at most 0.00095.
The roundings to bfloat16 on the way count: a program that leaves them out, or rounds other values in their place, can miss the bound.
Values may be sent and summed in bfloat16 or wider, within the bound.
A program may use at most 64 MiB of HBM per device.

v0:
```python
import math
import jax
import jax.numpy as jnp
from jax import lax
from jax.sharding import PartitionSpec as P

PB = 256
tomo_step = 1.0


def shifted(value, axis, steps):
    count = lax.axis_size(axis)
    leading, last = (max(0, -steps), min(count, count - steps))
    return lax.ppermute(value, axis, [(source, source + steps) for source in range(leading, last)])


def dft_tables(side):
    indices = jnp.arange(side, dtype=jnp.int32)
    products = indices[:, None] * indices[None, :] % side
    phase_angle = products.astype(jnp.float32) * (2.0 * math.pi / side)
    norm_factor = 1.0 / math.sqrt(side)
    return (
        (jnp.cos(phase_angle) * norm_factor).astype(jnp.bfloat16),
        (-jnp.sin(phase_angle) * norm_factor).astype(jnp.bfloat16),
    )


def matmul(left, right):
    return jnp.dot(left, right, preferred_element_type=jnp.float32)


def complex_matmul(left_real, left_imag, right_real, right_imag):
    out_real = matmul(left_real, right_real) - matmul(left_imag, right_imag)
    out_imag = matmul(left_real, right_imag) + matmul(left_imag, right_real)
    return (out_real, out_imag)


def patch_terms(patch_real, patch_imag, probe_real, probe_imag, amplitude, dft_real, dft_imag):
    wave_real = (probe_real * patch_real - probe_imag * patch_imag).astype(jnp.bfloat16)
    wave_imag = (probe_real * patch_imag + probe_imag * patch_real).astype(jnp.bfloat16)
    half_real, half_imag = complex_matmul(dft_real, dft_imag, wave_real, wave_imag)
    half_real = half_real.astype(jnp.bfloat16)
    half_imag = half_imag.astype(jnp.bfloat16)
    far_real, far_imag = complex_matmul(half_real, half_imag, dft_real, dft_imag)
    modulus = jnp.sqrt(far_real * far_real + far_imag * far_imag + 0.25)
    factor = amplitude.astype(jnp.float32) / modulus - 1.0
    diff_real = (far_real * factor).astype(jnp.bfloat16)
    diff_imag = (far_imag * factor).astype(jnp.bfloat16)
    conj_imag = -dft_imag
    back_half_real, back_half_imag = complex_matmul(dft_real, conj_imag, diff_real, diff_imag)
    back_half_real = back_half_real.astype(jnp.bfloat16)
    back_half_imag = back_half_imag.astype(jnp.bfloat16)
    back_real, back_imag = complex_matmul(back_half_real, back_half_imag, dft_real, conj_imag)
    object_real = probe_real * back_real + probe_imag * back_imag
    object_imag = probe_real * back_imag - probe_imag * back_real
    probe_grad_real = patch_real * back_real + patch_imag * back_imag
    probe_grad_imag = patch_real * back_imag - patch_imag * back_real
    energy = jnp.mean(patch_real * patch_real + patch_imag * patch_imag)
    return (
        jnp.stack([object_real, object_imag]),
        jnp.stack([probe_grad_real, probe_grad_imag]),
        energy,
    )


def tile_edges(values, offset):
    return shifted(values, "tile", offset)


def on_device(
    object_field,
    probe_field,
    amplitudes,
    pos_rows,
    pos_cols,
    counts,
    admm_dual,
    volume,
    proj_weights,
    ray_weights,
    angle_ids,
):
    half_side = PB // 2
    own_object = object_field[0]
    tile_cols = own_object.shape[2]
    from_left = tile_edges(own_object[:, :, tile_cols - half_side :], 1)
    from_right = tile_edges(own_object[:, :, :half_side], -1)
    extended = jnp.concatenate([from_left, own_object, from_right], axis=2)
    dft_real, dft_imag = dft_tables(PB)
    probe_real = probe_field[0]
    probe_imag = probe_field[1]
    zero_index = jnp.zeros((), jnp.int32)
    live_count = counts[0, 0]
    slot_total = amplitudes.shape[2]

    def slot_step(slot_index, state_tuple, weight):
        grad_sum, probe_sum, energy_sum = state_tuple
        anchor = (zero_index, pos_rows[0, 0, slot_index], pos_cols[0, 0, slot_index])
        object_patch = lax.dynamic_slice(extended, anchor, (2, PB, PB))
        object_part, probe_part, energy = patch_terms(
            object_patch[0],
            object_patch[1],
            probe_real,
            probe_imag,
            amplitudes[0, 0, slot_index],
            dft_real,
            dft_imag,
        )
        current = lax.dynamic_slice(grad_sum, anchor, (2, PB, PB))
        grad_sum = lax.dynamic_update_slice(grad_sum, current + weight * object_part, anchor)
        return (grad_sum, probe_sum + weight * probe_part, energy_sum + weight * energy)

    running = (
        jnp.zeros(extended.shape, jnp.float32),
        jnp.zeros((2, PB, PB), jnp.float32),
        jnp.zeros((), jnp.float32),
    )
    running = lax.fori_loop(
        0,
        slot_total,
        lambda slot_index, state_tuple: slot_step(
            slot_index, state_tuple, (slot_index < live_count).astype(jnp.float32)
        ),
        running,
    )
    grad_sum, probe_sum, energy_sum = running
    to_right_edge = tile_edges(grad_sum[:, :, :half_side], -1)
    to_left_edge = tile_edges(grad_sum[:, :, tile_cols + half_side :], 1)
    own_cells = grad_sum[:, :, half_side : half_side + tile_cols]
    own_cells = own_cells.at[:, :, :half_side].add(to_left_edge)
    own_cells = own_cells.at[:, :, tile_cols - half_side :].add(to_right_edge)
    probe_flat = jnp.concatenate([probe_sum.reshape(-1), jnp.broadcast_to(energy_sum, (128,))])
    probe_flat = lax.psum(probe_flat, ("tile", "proj", "cuts"))
    probe_grad = probe_flat[: probe_sum.size].reshape(probe_sum.shape)
    energy = probe_flat[probe_sum.size]
    new_probe = probe_field + probe_grad / (energy + 1e-05)
    probe_peak = jnp.max(probe_real * probe_real + probe_imag * probe_imag)
    new_object = (own_object + own_cells / (probe_peak + 1e-05))[None]
    slab_total = admm_dual.shape[1]
    first_row = (own_object.shape[1] - slab_total) // 2
    slab_values = new_object[:, 1, first_row : first_row + slab_total, :] + admm_dual
    arrived = lax.all_to_all(
        lax.all_to_all(slab_values, "proj", split_axis=2, concat_axis=0, tiled=True),
        "cuts",
        split_axis=1,
        concat_axis=0,
        tiled=True,
    )
    proj_count = lax.axis_size("proj")
    cuts_count = lax.axis_size("cuts")
    slab_dev = arrived.shape[1]
    u_share = arrived.shape[2]
    projections = proj_count * cuts_count
    arrived = arrived.reshape(cuts_count, proj_count, slab_dev, u_share).transpose(1, 0, 2, 3)
    target = (
        arrived.reshape(projections, slab_dev, u_share)
        .transpose(2, 0, 1)
        .reshape(u_share, projections * slab_dev)
    )
    angle_count = ray_weights.shape[0]
    x_share = volume.shape[1]
    width = volume.shape[2]
    onehot = (angle_ids[:, None] == jnp.arange(angle_count, dtype=jnp.int32)[None, :]).astype(
        jnp.float32
    )
    ray_table = jnp.dot(
        onehot, ray_weights, precision=lax.Precision.HIGHEST, preferred_element_type=jnp.float32
    )
    ray_sums = jnp.einsum("zxy,ay->azx", volume, ray_table, precision=lax.Precision.HIGHEST).astype(
        jnp.bfloat16
    )
    spread = onehot.astype(jnp.bfloat16)[:, :, None, None] * ray_sums[:, None, :, :]
    spread = spread.transpose(1, 3, 0, 2).reshape(angle_count * x_share, projections * slab_dev)
    weight_flat = proj_weights.reshape(angle_count * x_share, width)
    partial_term = lax.dot_general(
        weight_flat, spread, (((0,), (0,)), ((), ())), preferred_element_type=jnp.float32
    )
    own_rows = lax.psum_scatter(partial_term, ("tile", "proj"), scatter_dimension=0, tiled=True)
    own_residue = (own_rows - target).astype(jnp.bfloat16)
    residue = lax.all_gather(own_residue, ("tile", "proj"), axis=0, tiled=True)
    backproj = matmul(weight_flat, residue)
    backproj = backproj.reshape(angle_count, x_share, projections, slab_dev)
    back_sums = jnp.einsum("gxaz,ag->azx", backproj, onehot, precision=lax.Precision.HIGHEST)
    gradient = jnp.einsum("azx,ay->zxy", back_sums, ray_table, precision=lax.Precision.HIGHEST)
    new_volume = volume - tomo_step * gradient
    return (new_object, new_probe, new_volume)


def solution(mesh):
    in_specs = (
        P(("proj", "cuts"), None, None, "tile"),
        P(),
        P(("proj", "cuts"), "tile", None, None, None),
        P(("proj", "cuts"), "tile", None),
        P(("proj", "cuts"), "tile", None),
        P(("proj", "cuts"), "tile"),
        P(("proj", "cuts"), None, "tile"),
        P("cuts", ("tile", "proj"), None),
        P(None, ("tile", "proj"), None),
        P(),
        P(),
    )
    out_specs = (P(("proj", "cuts"), None, None, "tile"), P(), P("cuts", ("tile", "proj"), None))
    return jax.shard_map(
        on_device, mesh=mesh, in_specs=in_specs, out_specs=out_specs, check_vma=False
    )
```

profile of v0, /device:TPU:1, one launch (start us, length us, event | category | flops | bytes accessed | tf_op | source)
XLA Modules:
  0.0 628.5 jit_solution(16933225154168796481)
XLA Ops:
  8.1 3.2 copy.17
  13.5 4.0 collective-permute-start
  23.7 3.4 mul.431
  27.1 3.3 convolution_bitcast_fusion
  30.4 5.3 copy.31
  37.5 3.2 pad_maximum_fusion
  42.3 245.5 %while.23 = (s32[]{:T(128)}, f32[2,384,768]{1,2,0:T(8,128)}, f32[2,256,256]{2,1,0:T(8,128)}, f32[]{:T(128)}, s32[1,1,6]{2,1,0:T(1,128)S(1)}, /*index=5*/s32[1,1,...) while((s32[]{:T(128)}, f32[2,384,768]{1,2,0:T(8,128)}, ...), condition=%wide.region_2.3_spmd.clone.clone, body=%wide.region_0.2_spmd.clone.clone.sunk | while | flops 558956544 | bytes 21102956 | solution.py:118
  68.0 3.0 fusion.228
  75.4 6.6 %dynamic_update_slice.13 = f32[2,384,768]{1,2,0:T(8,128)} dynamic-update-slice(f32[2,384,768]{1,2,0:T(8,128)} %get-tuple-element.644, f32[2,256,256]{1,2,0:T(8,128)S(1)} %copy.50, s32[]{:T(128)} %constant.167.clone.1..sunk, s32[]{:T(128)S(6)} %select_n.153, s32[]{:T(128)S(6)} %select_n.154) | dynamic-update-slice | bytes 1048580 | tf_op jit(solution)/shard_map/while/body/eval_jaxpr/dynamic_update_slice | solution.py:110
  116.7 6.0 dynamic_update_slice.13
  157.4 6.2 dynamic_update_slice.13
  198.3 6.3 dynamic_update_slice.13
  239.3 6.6 %dynamic_update_slice.13 = f32[2,384,768]{1,2,0:T(8,128)} dynamic-update-slice(f32[2,384,768]{1,2,0:T(8,128)} %get-tuple-element.644, f32[2,256,256]{1,2,0:T(8,128)S(1)} %copy.50, s32[]{:T(128)} %constant.167.clone.1..sunk, s32[]{:T(128)S(6)} %select_n.153, s32[]{:T(128)S(6)} %select_n.154) | dynamic-update-slice | bytes 1048580 | tf_op jit(solution)/shard_map/while/body/eval_jaxpr/dynamic_update_slice | solution.py:110
  280.6 6.3 %dynamic_update_slice.13 = f32[2,384,768]{1,2,0:T(8,128)} dynamic-update-slice(f32[2,384,768]{1,2,0:T(8,128)} %get-tuple-element.644, f32[2,256,256]{1,2,0:T(8,128)S(1)} %copy.50, s32[]{:T(128)} %constant.167.clone.1..sunk, s32[]{:T(128)S(6)} %select_n.153, s32[]{:T(128)S(6)} %select_n.154) | dynamic-update-slice | bytes 1048580 | tf_op jit(solution)/shard_map/while/body/eval_jaxpr/dynamic_update_slice | solution.py:110
  289.7 5.9 collective-permute-start.2
  303.9 3.2 collective-permute-done.3
  313.5 22.6 %all_to_all.27 = f32[16,1,1024]{2,1,0:T(1,128)S(1)} all-to-all(f32[16,1,1024]{2,1,0:T(1,128)S(1)} %reshape.139), channel_id=1, replica_groups=mesh['tile'=4,'proj'=16,'cuts'=4] {'proj'}, dimensions={0} | all-to-all | bytes 131072 | tf_op jit(solution)/shard_map/all_to_all | solution.py:143
  340.0 3.3 all-to-all-start.1
  344.5 3.3 all-to-all-done.1
  348.8 102.0 %reduce-scatter.4.cloned.1.call-done = f32[32,512]{1,0:T(8,128)} async-done(((f32[2048,512]{1,0:T(8,128)}), f32[32,512]{1,0:T(8,128)}) %reduce-scatter.4.cloned.1.call-update) | async-done | bytes 65552
  452.6 145.6 %all-reduce.3.cloned.1.call-done = f32[131200]{0:T(1024)} async-done(((f32[131200]{0:T(1024)}), f32[131200]{0:T(1024)}) %all-reduce.3.cloned.1.call-update) | async-done | bytes 524816 | tf_op jit(solution)/shard_map/psum | solution.py:133
  604.0 3.0 copy.28
  612.4 3.8 fusion.126
  616.4 4.7 convolution_subtract_fusion.4
  (237 shorter events, 220.2 us)
Async XLA Ops:
  8.0 19.1 %copy-start = (bf16[16,32,2048]{2,1,0:T(8,128)(2,1)S(1)}, bf16[16,32,2048]{2,1,0:T(8,128)(2,1)}, u32[]{:S(2)}) copy-start(bf16[16,32,2048]{2,1,0:T(8,128)(2,1)} %param.25) | copy-start | bytes 6291460
  8.0 10.8 %copy-start.13 = (s32[64]{0:T(128)S(1)}, s32[64]{0:T(128)}, u32[]{:S(2)}) copy-start(s32[64]{0:T(128)} %param.27) | copy-start | bytes 772
  8.0 10.9 %copy-start.9 = (f32[16,2048]{1,0:T(8,128)S(1)}, f32[16,2048]{1,0:T(8,128)}, u32[]{:S(2)}) copy-start(f32[16,2048]{1,0:T(8,128)} %param.26) | copy-start | bytes 393220
  8.0 442.8 %reduce-scatter.4.cloned.1.call-start = ((), (), s32[]{:S(2)}) async-start(), calls=%async_computation.5 | async-start | bytes 4259840
  11.2 8.9 %copy-start.3 = (f32[8,32,2048]{2,1,0:T(8,128)S(1)}, f32[8,32,2048]{2,1,0:T(8,128)}, u32[]{:S(2)}) copy-start(f32[8,32,2048]{2,1,0:T(8,128)} %param.24) | copy-start | bytes 6291460
  13.5 24.0 %collective-permute-start = (f32[2,384,128]{1,2,0:T(8,128)}, f32[2,384,128]{1,2,0:T(8,128)S(1)}, u32[]{:S(2)}, u32[]{:S(2)}) collective-permute-start(f32[2,384,128]{1,2,0:T(8,128)} %get-tuple-element.528), channel_id=1, source_target_pairs={{0,64},{64,128},{128,192},{1,65},{65,129},{129,193},{2,66},{66,130... | collective-permute-start | bytes 1179656 | tf_op jit(solution)/shard_map/ppermute | solution.py:14
  17.6 19.9 %collective-permute-start.1 = (f32[2,384,128]{1,2,0:T(8,128)}, f32[2,384,128]{1,2,0:T(8,128)}, u32[]{:S(2)}, u32[]{:S(2)}) collective-permute-start(f32[2,384,128]{1,2,0:T(8,128)} %get-tuple-element.529), channel_id=1, source_target_pairs={{64,0},{128,64},{192,128},{65,1},{129,65},{193,129},{66,2},{130,66... | collective-permute-start | bytes 1179656 | tf_op jit(solution)/shard_map/ppermute | solution.py:14
  19.4 0.8 copy-start.7
  35.7 1.0 copy-start.5
  40.7 1.6 copy-start.11
  40.7 1.6 copy-start.12
  42.2 254.7 %copy-start.10 = (f32[1,32,512]{2,1,0:T(8,128)S(1)}, f32[1,32,512]{2,1,0:T(8,128)}, u32[]{:S(2)}) copy-start(f32[1,32,512]{2,1,0:T(8,128)} %param.23) | copy-start | bytes 196612
  287.7 9.4 %copy-start.6 = (f32[2,256,256]{2,1,0:T(8,128)S(1)}, f32[2,256,256]{2,1,0:T(8,128)}, u32[]{:S(2)}) copy-start(f32[2,256,256]{2,1,0:T(8,128)} %param.18) | copy-start | bytes 1572868
  289.7 13.1 %collective-permute-start.2 = (f32[2,384,128]{1,2,0:T(8,128)}, f32[2,384,128]{1,2,0:T(8,128)}, u32[]{:S(2)}, u32[]{:S(2)}) collective-permute-start(f32[2,384,128]{1,2,0:T(8,128)} %get-tuple-element.527), channel_id=1, source_target_pairs={{0,64},{64,128},{128,192},{1,65},{65,129},{129,193},{2,66},{66,130... | collective-permute-start | bytes 1179656 | tf_op jit(solution)/shard_map/ppermute | solution.py:14
  295.7 11.4 %collective-permute-start.3 = (f32[2,384,128]{1,2,0:T(8,128)S(1)}, f32[2,384,128]{1,2,0:T(8,128)}, u32[]{:S(2)}, u32[]{:S(2)}) collective-permute-start(f32[2,384,128]{1,2,0:T(8,128)S(1)} %get-tuple-element.526), channel_id=1, source_target_pairs={{64,0},{128,64},{192,128},{65,1},{129,65},{193,129},{66,2},{130,66... | collective-permute-start | bytes 1179656 | tf_op jit(solution)/shard_map/ppermute | solution.py:14
  298.4 9.8 %copy-start.1 = (f32[1,2,384,512]{2,3,1,0:T(8,128)S(1)}, f32[1,2,384,512]{2,3,1,0:T(8,128)}, u32[]{:S(2)}) copy-start(f32[1,2,384,512]{2,3,1,0:T(8,128)} %copy.17) | copy-start | bytes 4718596
  308.4 1.1 copy-start.4
  309.5 33.8 %copy-start.2 = (f32[2,256,256]{2,1,0:T(8,128)S(1)}, f32[2,256,256]{2,1,0:T(8,128)}, u32[]{:S(2)}) copy-start(f32[2,256,256]{2,1,0:T(8,128)} %get-tuple-element.383) | copy-start | bytes 1572868
  340.0 7.9 %all-to-all-start.1 = ((f32[4,1,4096]{2,1,0:T(1,128)}), f32[4,1,4096]{2,1,0:T(1,128)S(1)}, u32[]{:S(2)}, u32[]{:S(2)}) async-start(f32[4,1,4096]{2,1,0:T(1,128)} %reshape.141), calls=%async_computation.1 | async-start | bytes 131072 | tf_op jit(solution)/shard_map/all_to_all | solution.py:142
  343.3 254.9 %all-reduce.3.cloned.1.call-start = ((), (), s32[]{:S(2)}) async-start(), calls=%async_computation.3 | async-start | bytes 1056768 | tf_op jit(solution)/shard_map/psum | solution.py:133
  344.5 262.5 %all-gather.2.cloned.1.call-start = ((), (), s32[]{:S(2)}) async-start(), calls=%async_computation.4 | async-start | bytes 2129920 | tf_op jit(solution)/shard_map/all_gather | solution.py:180
  612.4 4.0 copy-start.8
Sparse Core Ops, SparseCore 0:
  35.8 414.9 reduce-scatter.3
  454.3 86.0 all-gather.1
Sparse Core Ops, SparseCore 1:
  349.8 248.3 all-reduce.2
where the time goes:
time: 632 us; the launch traced here: 629 us
  waiting for transfers between devices  257 us (41%)
  matrix products  143 us (23%)
  local copies, waits for them, and re-layouts  99.8 us (16%)
  other arithmetic  42.6 us (7%)
  loops' own time  30.5 us (5%)
  blocking collectives  22.6 us (4%)
  between operations  17.1 us (3%)
  starting transfers between devices  16 us (3%)
    psum x1, waiting for transfers between devices, on_device(): probe_flat = lax.psum(probe_flat, ('tile', 'proj', 'cuts'))  146 us
    dot_general x97, matrix products, matmul(): return jnp.dot(left, right, preferred_element_type=jnp.float32)  129 us
    unnamed x4, waiting for transfers between devices  102 us
    dynamic_update_slice x12, local copies, waits for them, and re-layouts, slot_step(): lax.dynamic_update_slice(grad_sum, current + weight * object_part, anchor)  39.1 us
    another operation x1, loops' own time, on_device(): lax.fori_loop(0, slot_total, lambda slot_index, state_tuple: slot_step(sl...  30.5 us
    all_to_all x1, blocking collectives, on_device(): lax.all_to_all(slab_values, 'proj', split_axis=2, concat_axis=0, tiled=True)  22.6 us
    unnamed x40, local copies, waits for them, and re-layouts  18.8 us
  transfers between devices with their start and end apart: 8, of which 5 were waited for; matrix products, arithmetic and copies ran while one was open for 42% of the time, Pallas kernels for 0%

commit v1 on v0

--- a/solution.py
+++ b/solution.py
@@ -130,7 +130,7 @@
     own_cells = own_cells.at[:, :, :half_side].add(to_left_edge)
     own_cells = own_cells.at[:, :, tile_cols - half_side :].add(to_right_edge)
     probe_flat = jnp.concatenate([probe_sum.reshape(-1), jnp.broadcast_to(energy_sum, (128,))])
-    probe_flat = lax.psum(probe_flat, ("tile", "proj", "cuts"))
+    probe_flat = lax.psum(lax.psum(probe_flat, ("proj", "cuts")), "tile")
     probe_grad = probe_flat[: probe_sum.size].reshape(probe_sum.shape)
     energy = probe_flat[probe_sum.size]
     new_probe = probe_field + probe_grad / (energy + 1e-05)

time: 632 us -> 823 us (1.30)
  waiting for transfers between devices: 257 us -> 446 us
  starting transfers between devices: 16 us -> 25.9 us
  blocking collectives: 22.6 us -> 13.7 us
    unnamed x4 -> x5, waiting for transfers between devices: 102 us -> 219 us
    all_gather x1, waiting for transfers between devices: 0.01 us -> 78 us  [on_device(): residue = lax.all_gather(own_residue, ('tile', 'proj'), axis=0, tiled=True)]
    all_to_all x1, starting transfers between devices: 3.28 us -> 13 us  [on_device(): lax.all_to_all(slab_values, 'proj', split_axis=2, concat_axis=0, tiled=True)]
    all_to_all x1, blocking collectives: 22.6 us -> 13.7 us  [on_device(): lax.all_to_all(lax.all_to_all(slab_values, 'proj', split_axis=2, concat_a...]
    psum x1 -> x2, waiting for transfers between devices: 146 us -> 143 us  [on_device(): probe_flat = lax.psum(lax.psum(probe_flat, ('proj', 'cuts')), 'tile')]
    unnamed x40 -> x38, local copies, waits for them, and re-layouts: 18.8 us -> 18.1 us
  transfers between devices with their start and end apart: 8 -> 9, of which waited for: 5 -> 5; matrix products, arithmetic and copies ran while one was open for 42% -> 5% of each run, Pallas kernels for 0% -> 0%
where the time goes in v1:
time: 823 us; the launch traced here: 820 us
  waiting for transfers between devices  446 us (54%)
  matrix products  145 us (18%)
  local copies, waits for them, and re-layouts  99.1 us (12%)
  other arithmetic  40.9 us (5%)
  loops' own time  32.5 us (4%)
  starting transfers between devices  25.9 us (3%)
  between operations  17.1 us (2%)
  blocking collectives  13.7 us (2%)
    unnamed x5, waiting for transfers between devices  219 us
    psum x2, waiting for transfers between devices, on_device(): probe_flat = lax.psum(lax.psum(probe_flat, ('proj', 'cuts')), 'tile')  143 us
    dot_general x97, matrix products, matmul(): return jnp.dot(left, right, preferred_element_type=jnp.float32)  129 us
    all_gather x1, waiting for transfers between devices, on_device(): residue = lax.all_gather(own_residue, ('tile', 'proj'), axis=0, tiled=True)  78 us
    dynamic_update_slice x12, local copies, waits for them, and re-layouts, slot_step(): lax.dynamic_update_slice(grad_sum, current + weight * object_part, anchor)  39 us
    another operation x1, loops' own time, on_device(): lax.fori_loop(0, slot_total, lambda slot_index, state_tuple: slot_step(sl...  32.5 us
    unnamed x38, local copies, waits for them, and re-layouts  18.1 us
  transfers between devices with their start and end apart: 9, of which 5 were waited for; matrix products, arithmetic and copies ran while one was open for 5% of the time, Pallas kernels for 0%

profile of v1, /device:TPU:1, one launch (start us, length us, event | category | flops | bytes accessed | tf_op | source)
XLA Modules:
  0.0 819.8 jit_solution(4945872668138544984)
XLA Ops:
  8.1 3.2 copy.17
  13.3 4.0 collective-permute-start
  20.0 3.4 fusion.122
  25.1 4.1 mul.431
  29.9 3.1 pad_maximum_fusion
  34.7 247.7 %while.23 = (s32[]{:T(128)}, f32[2,384,768]{1,2,0:T(8,128)}, f32[2,256,256]{2,1,0:T(8,128)}, f32[]{:T(128)}, s32[1,1,6]{2,1,0:T(1,128)S(1)}, /*index=5*/s32[1,1,...) while((s32[]{:T(128)}, f32[2,384,768]{1,2,0:T(8,128)}, ...), condition=%wide.region_2.3_spmd.clone.clone, body=%wide.region_0.2_spmd.clone.clone.sunk | while | flops 558956544 | bytes 21102956 | solution.py:118
  68.2 6.5 dynamic_update_slice.13
  109.8 6.0 dynamic_update_slice.13
  150.9 6.2 dynamic_update_slice.13
  192.2 6.3 dynamic_update_slice.13
  233.6 6.5 dynamic_update_slice.13
  275.3 6.3 dynamic_update_slice.13
  284.8 3.2 convolution_bitcast_fusion
  288.0 5.4 copy.31
  295.4 6.1 collective-permute-start.2
  309.7 3.2 collective-permute-done.3
  318.4 13.0 %all-to-all-start = ((f32[16,1,1024]{2,1,0:T(1,128)}), f32[16,1,1024]{2,1,0:T(1,128)S(1)}, u32[]{:S(2)}, u32[]{:S(2)}) async-start(f32[16,1,1024]{2,1,0:T(1,128)} %reshape.139), calls=%async_computation | async-start | bytes 131072 | tf_op jit(solution)/shard_map/all_to_all | solution.py:143
  331.4 142.9 %all-reduce.4.cloned.1.call-done = f32[131200]{0:T(1024)} async-done(((f32[131200]{0:T(1024)}), f32[131200]{0:T(1024)}) %all-reduce.4.cloned.1.call-update) | async-done | bytes 524816 | tf_op jit(solution)/shard_map/psum | solution.py:133
  476.0 13.7 %all_to_all.27 = f32[4,1,4096]{2,1,0:T(1,128)S(1)} all-to-all(f32[4,1,4096]{2,1,0:T(1,128)S(1)} %reshape.141), channel_id=1, replica_groups=mesh['tile'=4,'proj'=16,'cuts'=4] {'cuts'}, dimensions={0} | all-to-all | bytes 131072 | tf_op jit(solution)/shard_map/all_to_all | solution.py:142
  490.7 219.0 %reduce-scatter.4.cloned.1.call-done = f32[32,512]{1,0:T(8,128)} async-done(((f32[2048,512]{1,0:T(8,128)}), f32[32,512]{1,0:T(8,128)}) %reduce-scatter.4.cloned.1.call-update) | async-done | bytes 65552
  711.5 3.0 copy.28
  720.3 78.0 %all-gather.2.cloned.1.call-done = bf16[2048,512]{1,0:T(8,128)(2,1)} async-done(((bf16[32,512]{1,0:T(8,128)(2,1)}), bf16[2048,512]{1,0:T(8,128)(2,1)}) %all-gather.2.cloned.1.call-update) | async-done | bytes 2097168 | tf_op jit(solution)/shard_map/all_gather | solution.py:180
  803.7 3.8 fusion.126
  807.7 4.7 convolution_subtract_fusion.4
  (238 shorter events, 218.6 us)
Async XLA Ops:
  8.0 276.7 %copy-start = (bf16[16,32,2048]{2,1,0:T(8,128)(2,1)S(1)}, bf16[16,32,2048]{2,1,0:T(8,128)(2,1)}, u32[]{:S(2)}) copy-start(bf16[16,32,2048]{2,1,0:T(8,128)(2,1)} %param.25) | copy-start | bytes 6291460
  8.0 10.7 %copy-start.12 = (s32[64]{0:T(128)S(1)}, s32[64]{0:T(128)}, u32[]{:S(2)}) copy-start(s32[64]{0:T(128)} %param.27) | copy-start | bytes 772
  8.0 10.7 %copy-start.8 = (f32[16,2048]{1,0:T(8,128)S(1)}, f32[16,2048]{1,0:T(8,128)}, u32[]{:S(2)}) copy-start(f32[16,2048]{1,0:T(8,128)} %param.26) | copy-start | bytes 393220
  8.0 466.3 %all-reduce.4.cloned.1.call-start = ((), (), s32[]{:S(2)}) async-start(), calls=%async_computation.3 | async-start | bytes 1056768 | tf_op jit(solution)/shard_map/psum | solution.py:133
  13.3 16.6 %collective-permute-start = (f32[2,384,128]{1,2,0:T(8,128)}, f32[2,384,128]{1,2,0:T(8,128)S(1)}, u32[]{:S(2)}, u32[]{:S(2)}) collective-permute-start(f32[2,384,128]{1,2,0:T(8,128)} %get-tuple-element.528), channel_id=1, source_target_pairs={{0,64},{64,128},{128,192},{1,65},{65,129},{129,193},{2,66},{66,130... | collective-permute-start | bytes 1179656 | tf_op jit(solution)/shard_map/ppermute | solution.py:14
  17.4 12.6 %collective-permute-start.1 = (f32[2,384,128]{1,2,0:T(8,128)}, f32[2,384,128]{1,2,0:T(8,128)}, u32[]{:S(2)}, u32[]{:S(2)}) collective-permute-start(f32[2,384,128]{1,2,0:T(8,128)} %get-tuple-element.529), channel_id=1, source_target_pairs={{64,0},{128,64},{192,128},{65,1},{129,65},{193,129},{66,2},{130,66... | collective-permute-start | bytes 1179656 | tf_op jit(solution)/shard_map/ppermute | solution.py:14
  19.2 0.8 copy-start.5
  23.5 5.7 copy-start.3
  33.1 1.6 copy-start.10
  33.1 1.6 copy-start.11
  282.5 2.3 copy-start.7
  284.7 425.0 %reduce-scatter.4.cloned.1.call-start = ((), (), s32[]{:S(2)}) async-start(), calls=%async_computation.6 | async-start | bytes 4259840
  293.4 9.4 %copy-start.9 = (f32[1,32,512]{2,1,0:T(8,128)S(1)}, f32[1,32,512]{2,1,0:T(8,128)}, u32[]{:S(2)}) copy-start(f32[1,32,512]{2,1,0:T(8,128)} %param.23) | copy-start | bytes 196612
  293.4 9.5 %copy-start.4 = (f32[2,256,256]{2,1,0:T(8,128)S(1)}, f32[2,256,256]{2,1,0:T(8,128)}, u32[]{:S(2)}) copy-start(f32[2,256,256]{2,1,0:T(8,128)} %param.18) | copy-start | bytes 1572868
  295.4 13.2 %collective-permute-start.2 = (f32[2,384,128]{1,2,0:T(8,128)}, f32[2,384,128]{1,2,0:T(8,128)}, u32[]{:S(2)}, u32[]{:S(2)}) collective-permute-start(f32[2,384,128]{1,2,0:T(8,128)} %get-tuple-element.527), channel_id=1, source_target_pairs={{0,64},{64,128},{128,192},{1,65},{65,129},{129,193},{2,66},{66,130... | collective-permute-start | bytes 1179656 | tf_op jit(solution)/shard_map/ppermute | solution.py:14
  301.5 11.5 %collective-permute-start.3 = (f32[2,384,128]{1,2,0:T(8,128)S(1)}, f32[2,384,128]{1,2,0:T(8,128)}, u32[]{:S(2)}, u32[]{:S(2)}) collective-permute-start(f32[2,384,128]{1,2,0:T(8,128)S(1)} %get-tuple-element.526), channel_id=1, source_target_pairs={{64,0},{128,64},{192,128},{65,1},{129,65},{193,129},{66,2},{130,66... | collective-permute-start | bytes 1179656 | tf_op jit(solution)/shard_map/ppermute | solution.py:14
  304.2 9.8 %copy-start.1 = (f32[1,2,384,512]{2,3,1,0:T(8,128)S(1)}, f32[1,2,384,512]{2,3,1,0:T(8,128)}, u32[]{:S(2)}) copy-start(f32[1,2,384,512]{2,3,1,0:T(8,128)} %copy.17) | copy-start | bytes 4718596
  314.2 1.1 copy-start.2
  318.4 156.0 %all-to-all-start = ((f32[16,1,1024]{2,1,0:T(1,128)}), f32[16,1,1024]{2,1,0:T(1,128)S(1)}, u32[]{:S(2)}, u32[]{:S(2)}) async-start(f32[16,1,1024]{2,1,0:T(1,128)} %reshape.139), calls=%async_computation | async-start | bytes 131072 | tf_op jit(solution)/shard_map/all_to_all | solution.py:143
  331.4 383.2 %all-reduce.6.cloned.1.call-start = ((), (), s32[]{:S(2)}) async-start(), calls=%async_computation.4 | async-start | bytes 1056768 | tf_op jit(solution)/shard_map/psum | solution.py:133
  474.3 324.0 %all-gather.2.cloned.1.call-start = ((), (), s32[]{:S(2)}) async-start(), calls=%async_computation.5 | async-start | bytes 2129920 | tf_op jit(solution)/shard_map/all_gather | solution.py:180
  803.7 4.0 copy-start.6
Sparse Core Ops, SparseCore 0:
  284.8 189.4 all-reduce.3
  476.6 47.1 all-reduce.5
Sparse Core Ops, SparseCore 1:
  293.5 416.2 reduce-scatter.3
  713.1 85.2 all-gather.1
